TPU v7x, 512 devices: a whole 4x8x8 slice. The times are simulated.
512 devices in a mesh: region: 32 (over x, y), band: 16 (over z, core).
Axes of the slice: x: 4, y: 8, z: 8, core: 2. Of those that a mesh axis runs over, the one named last changes fastest.
Arguments:
- vertex_inputs: bfloat16 [131072, 512], P(('region', 'band')), may hold values from -20 to 20
- partition_embed_matrix: bfloat16 [512, 512], replicated, may hold values from -0.25 to 0.25
- selector_embed_matrix: bfloat16 [512, 512], replicated, may hold values from -0.25 to 0.25
- partition_affinity_matrix: bfloat16 [64, 64], replicated, may hold values from -0.75 to 0.75
- sharpness_divisor: float32 [8], replicated, may hold values from 0.5 to 2
- latent_query_key_value_maps: float32 [3, 64, 64], replicated, may hold values from -0.75 to 0.75
- result_cotangent: bfloat16 [131072, 512], P(('region', 'band')), may hold values from -6 to 6
Outputs:
- grad_points: bfloat16 [131072, 512], P(('region', 'band'))
- grad_proj: float32 [512, 1024], P('region')
- grad_w_slice: float32 [64, 64], replicated
- grad_w_token: float32 [3, 64, 64], replicated
All inputs are finite; a program needn't handle non-finite values.
Results may differ from a plain program's by a relative error of at most 0.013.
The roundings to bfloat16 on the way count: a program that leaves them out, or rounds other values in their place, can miss the bound.
Values sent between devices are 32-bit elements; how exact they have to be, the bound alone decides.
A program may use at most 64 MiB of HBM per device.

v0:
```python
import math

import jax
import jax.numpy as jnp
from jax import lax
from jax.sharding import PartitionSpec as P

partition_affinity_bound = 8.0
score_cap = 10.0
epsilon = 1e-05


def token_mix(tokens, latent_query_key_value_maps):
    highest = lax.Precision.HIGHEST
    head_width = tokens.shape[2]
    queries = jnp.einsum("hgc,cd->hgd", tokens, latent_query_key_value_maps[0], precision=highest)
    key_rows = jnp.einsum("hgc,cd->hgd", tokens, latent_query_key_value_maps[1], precision=highest)
    values = jnp.einsum("hgc,cd->hgd", tokens, latent_query_key_value_maps[2], precision=highest)
    scores = jnp.einsum("hgd,hkd->hgk", queries, key_rows, precision=highest) / math.sqrt(
        head_width
    )
    capped = score_cap * jnp.tanh(scores / score_cap)
    exp_scores = jnp.exp(capped)
    attention = exp_scores / jnp.sum(exp_scores, axis=-1, keepdims=True)
    mixing = jnp.einsum("hgk,hkd->hgd", attention, values, precision=highest)
    return tokens + mixing


def body(
    vertex_inputs,
    partition_embed_matrix,
    selector_embed_matrix,
    partition_affinity_matrix,
    sharpness_divisor,
    latent_query_key_value_maps,
    result_cotangent,
):
    local_rows = vertex_inputs.shape[0]
    attn_group_index = sharpness_divisor.shape[0]
    head_width = partition_affinity_matrix.shape[0]
    slice_count = partition_affinity_matrix.shape[1]
    feature = jnp.dot(
        vertex_inputs, partition_embed_matrix, preferred_element_type=jnp.float32
    ).astype(jnp.bfloat16)
    middle = jnp.dot(
        vertex_inputs, selector_embed_matrix, preferred_element_type=jnp.float32
    ).astype(jnp.bfloat16)
    middle_heads = middle.reshape(local_rows, attn_group_index, head_width)
    feature_heads = feature.reshape(local_rows, attn_group_index, head_width)
    grad_heads = result_cotangent.reshape(local_rows, attn_group_index, head_width)
    unclamped_attention_affinity = jnp.einsum(
        "nhc,cg->nhg", middle_heads, partition_affinity_matrix, preferred_element_type=jnp.float32
    )
    smooth_clamping_function = jnp.tanh(
        unclamped_attention_affinity / (partition_affinity_bound * sharpness_divisor[None, :, None])
    )
    exp_logit = jnp.exp(partition_affinity_bound * smooth_clamping_function)
    weight = exp_logit / jnp.sum(exp_logit, axis=-1, keepdims=True)
    weight_b = weight.astype(jnp.bfloat16)
    mass_part = jnp.sum(weight, axis=0).T
    token_part = jnp.einsum(
        "nhg,nhc->ghc", weight_b, feature_heads, preferred_element_type=jnp.float32
    ).reshape(slice_count, attn_group_index * head_width)
    back_part = jnp.einsum(
        "nhg,nhc->ghc", weight_b, grad_heads, preferred_element_type=jnp.float32
    ).reshape(slice_count, attn_group_index * head_width)
    slice_mass, token_sum, back_sum = lax.psum(
        (mass_part, token_part, back_part), ("region", "band")
    )
    denominator = slice_mass.T + epsilon
    token_heads = token_sum.reshape(slice_count, attn_group_index, head_width).transpose(1, 0, 2)
    back_heads = back_sum.reshape(slice_count, attn_group_index, head_width).transpose(1, 0, 2)
    tokens = token_heads / denominator[:, :, None]
    out_token, pullback = jax.vjp(token_mix, tokens, latent_query_key_value_maps)
    grad_token, grad_w_token = pullback(back_heads)
    out_b = out_token.astype(jnp.bfloat16)
    grad_sum_b = (grad_token / denominator[:, :, None]).astype(jnp.bfloat16)
    grad_mass = -jnp.sum(grad_token * tokens, axis=-1) / denominator
    grad_weight = jnp.einsum("nhc,hgc->nhg", grad_heads, out_b, preferred_element_type=jnp.float32)
    grad_weight = grad_weight + jnp.einsum(
        "nhc,hgc->nhg", feature_heads, grad_sum_b, preferred_element_type=jnp.float32
    )
    grad_weight = grad_weight + grad_mass[None]
    preactivation_cotangent = weight * (
        grad_weight - jnp.sum(weight * grad_weight, axis=-1, keepdims=True)
    )
    unprocessed_cotangent = (
        preactivation_cotangent
        * (1.0 - smooth_clamping_function * smooth_clamping_function)
        / sharpness_divisor[None, :, None]
    ).astype(jnp.bfloat16)
    grad_feature = (
        jnp.einsum("nhg,hgc->nhc", weight_b, grad_sum_b, preferred_element_type=jnp.float32)
        .reshape(local_rows, attn_group_index * head_width)
        .astype(jnp.bfloat16)
    )
    grad_mid = (
        jnp.einsum(
            "nhg,cg->nhc",
            unprocessed_cotangent,
            partition_affinity_matrix,
            preferred_element_type=jnp.float32,
        )
        .reshape(local_rows, attn_group_index * head_width)
        .astype(jnp.bfloat16)
    )
    grad_points = jnp.dot(
        grad_feature, partition_embed_matrix.T, preferred_element_type=jnp.float32
    )
    grad_points = (
        grad_points + jnp.dot(grad_mid, selector_embed_matrix.T, preferred_element_type=jnp.float32)
    ).astype(jnp.bfloat16)
    grad_joined = jnp.concatenate([grad_feature, grad_mid], axis=1)
    slice_part = jnp.einsum(
        "nhc,nhg->cg", middle_heads, unprocessed_cotangent, preferred_element_type=jnp.float32
    )
    proj_part = lax.dot_general(
        vertex_inputs, grad_joined, (((0,), (0,)), ((), ())), preferred_element_type=jnp.float32
    )
    grad_w_slice, full_proj = lax.psum((slice_part, proj_part), ("region", "band"))
    row_share = full_proj.shape[0] // lax.axis_size("region")
    grad_proj = lax.dynamic_slice_in_dim(
        full_proj, lax.axis_index("region") * row_share, row_share, 0
    )
    return (grad_points, grad_proj, grad_w_slice, grad_w_token)


def solution(mesh):
    return jax.shard_map(
        body,
        mesh=mesh,
        in_specs=(
            P(("region", "band"), None),
            P(),
            P(),
            P(),
            P(),
            P(),
            P(("region", "band"), None),
        ),
        out_specs=(P(("region", "band"), None), P("region", None), P(), P()),
        check_vma=False,
    )
```

profile of v0, /device:TPU:1, one launch (start us, length us, event | category | flops | bytes accessed | tf_op | source)
XLA Modules:
  0.0 683.9 jit_solution(16403802453781670062)
XLA Ops:
  7.3 0.7 broadcast_multiply_fusion
  8.0 1.1 copy.29
  9.1 1.2 convolution_convert_fusion.2
  11.4 0.9 fusion.55
  12.3 0.9 fusion.57
  13.5 107.8 %psum.37 = f32[64,8]{0,1:T(8,128)S(1)} all-reduce(f32[64,8]{0,1:T(8,128)S(1)} %bitcast.95), channel_id=1, replica_groups=mesh['region'=32,'band'=16] {'region','band'}, use_global_device_ids=true, to_apply=%region_4.0 | all-reduce | flops 512 | bytes 4096 | tf_op jit(solution)/shard_map/psum | solution.py:67
  121.3 168.2 %all-reduce.9.cloned.1.call-done = (f32[8,64,64]{2,1,0:T(8,128)}, f32[8,64,64]{2,1,0:T(8,128)}) async-done(((f32[8,64,64]{2,1,0:T(8,128)}, f32[8,64,64]{2,1,0:T(8,128)}), (f32[8,64,64]{2,1,0:T(8,128)}, f32[8,64,64]{2,1,0:T(8,128)})) %all-reduce.9.cloned.1.call-update) | async-done | bytes 262160 | tf_op jit(solution)/shard_map/psum | solution.py:67
  289.5 1.4 fusion.34
  290.9 1.4 fusion.30
  292.3 1.4 fusion.37
  293.7 0.6 fusion.26
  294.3 0.6 fusion.11
  295.5 0.7 fusion.59
  297.5 0.7 convolution_bitcast_fusion.3
  299.6 1.4 convolution_bitcast_fusion.4
  301.8 97.4 %psum.39 = f32[64,64]{1,0:T(8,128)} all-reduce(f32[64,64]{1,0:T(8,128)S(1)} %convolution_bitcast_fusion.4), channel_id=1, replica_groups=mesh['region'=32,'band'=16] {'region','band'}, use_global_device_ids=true, to_apply=%region_10.0 | all-reduce | flops 4096 | bytes 32768 | tf_op jit(solution)/shard_map/psum | solution.py:120
  399.1 1.7 convolution_bitcast_fusion
  400.9 0.7 convolution_bitcast_fusion.2
  401.8 0.7 convolution_bitcast_fusion.1
  402.5 0.7 pad_add_fusion
  403.5 1.1 fusion.8
  404.6 270.4 %all-reduce.7.cloned.1.call-done = f32[512,1024]{0,1:T(8,128)} async-done(((f32[512,1024]{0,1:T(8,128)}), f32[512,1024]{0,1:T(8,128)}) %all-reduce.7.cloned.1.call-update) | async-done | bytes 2097168 | tf_op jit(solution)/shard_map/psum | solution.py:120
  675.0 1.2 constant_dynamic-slice_fusion
  676.2 0.8 copy.39
  (48 shorter events, 5.8 us)
Async XLA Ops:
  7.2 1.9 copy-start
  7.2 3.3 copy-start.1
  7.2 3.3 copy-start.2
  7.2 3.8 copy-start.10
  7.2 282.2 %all-reduce.9.cloned.1.call-start = ((), (), s32[]{:S(2)}) async-start(), calls=%async_computation.1 | async-start | bytes 1048576 | tf_op jit(solution)/shard_map/psum | solution.py:67
  11.0 1.3 copy-start.4
  12.3 277.2 %copy-start.9 = (f32[3,64,64]{2,1,0:T(8,128)S(1)}, f32[3,64,64]{2,1,0:T(8,128)}, u32[]{:S(2)}) copy-start(f32[3,64,64]{2,1,0:T(8,128)} %param.12) | copy-start | bytes 147460
  13.2 661.7 %all-reduce.7.cloned.1.call-start = ((), (), s32[]{:S(2)}) async-start(), calls=%async_computation | async-start | bytes 4194304 | tf_op jit(solution)/shard_map/psum | solution.py:120
  289.5 4.9 copy-start.5
  290.9 4.0 copy-start.3
  296.2 2.4 copy-start.7
  298.2 1.4 copy-start.11
  399.1 1.8 copy-start.6
  400.9 0.9 copy-start.8
Sparse Core Ops, SparseCore 0:
  13.8 275.6 all-reduce.8
  401.0 273.9 all-reduce.6
where the time goes:
time: 684 us
  waiting for transfers between devices  439 us (64%)
  blocking collectives  205 us (30%)
  matrix products  20.3 us (3%)
  between operations  14.4 us (2%)
    psum x1, waiting for transfers between devices, body(): lax.psum((slice_part, proj_part), ('region', 'band'))  270 us
    psum x1, waiting for transfers between devices, body(): lax.psum((mass_part, token_part, back_part), ('region', 'band'))  168 us
    psum x1, blocking collectives, body(): lax.psum((mass_part, token_part, back_part), ('region', 'band'))  108 us
    psum x1, blocking collectives, body(): lax.psum((slice_part, proj_part), ('region', 'band'))  97.4 us
  transfers between devices with their start and end apart: 2, of which 2 were waited for; matrix products, arithmetic and copies ran while one was open for 1% of the time, Pallas kernels for 0%

commit v1 on v0

--- a/solution.py
+++ b/solution.py
@@ -3,11 +3,16 @@
 import jax
 import jax.numpy as jnp
 from jax import lax
+from jax.experimental import pallas as pl
+from jax.experimental.pallas import tpu as pltpu
 from jax.sharding import PartitionSpec as P
 
 partition_affinity_bound = 8.0
 score_cap = 10.0
 epsilon = 1e-05
+
+NX, NY, NZ = 4, 8, 8
+MESH = pl.DeviceIdType.MESH
 
 
 def token_mix(tokens, latent_query_key_value_maps):
@@ -24,6 +29,252 @@
     attention = exp_scores / jnp.sum(exp_scores, axis=-1, keepdims=True)
     mixing = jnp.einsum("hgk,hkd->hgd", attention, values, precision=highest)
     return tokens + mixing
+
+
+class Place:
+    def __init__(self):
+        region, band = lax.axis_index("region"), lax.axis_index("band")
+        self.x, self.y = lax.div(region, NY), lax.rem(region, NY)
+        self.z, self.c = lax.div(band, 2), lax.rem(band, 2)
+
+    def device(self, x=None, y=None, z=None, c=None):
+        x = self.x if x is None else x
+        y = self.y if y is None else y
+        z = self.z if z is None else z
+        c = self.c if c is None else c
+        return {"region": x * NY + y, "band": z * 2 + c}
+
+    def along(self, axis):
+        size = {"x": NX, "y": NY, "z": NZ}[axis]
+        here = getattr(self, axis)
+        order = sorted(range(1, size), key=lambda k: -min(k, size - k))
+        for k in order:
+            there = lax.rem(here + k, size)
+            yield k, there, self.device(**{axis: there})
+
+    def greet(self):
+        barrier = pltpu.get_barrier_semaphore()
+        count = 0
+        partners = [self.device(c=1 - self.c)]
+        for axis in "xyz":
+            partners += [d for _, _, d in self.along(axis)]
+        for d in partners:
+            pl.semaphore_signal(barrier, inc=1, device_id=d, device_id_type=MESH)
+            count += 1
+        pl.semaphore_wait(barrier, count)
+
+
+class Sends:
+    def __init__(self, send_sem, recv_sem):
+        self.send_sem, self.recv_sem, self.used, self.open = send_sem, recv_sem, 0, []
+
+    def start(self, src, dst, device):
+        i = self.used
+        self.used += 1
+        copy = pltpu.make_async_remote_copy(
+            src_ref=src,
+            dst_ref=dst,
+            send_sem=self.send_sem.at[i],
+            recv_sem=self.recv_sem.at[i],
+            device_id=device,
+            device_id_type=MESH,
+        )
+        copy.start()
+        self.open.append(copy)
+        return copy
+
+    def recv(self, copies):
+        for copy in copies:
+            copy.wait_recv()
+
+    def finish(self):
+        for copy in self.open:
+            copy.wait_send()
+
+
+def total_kernel(part, mass, full_out, mass_out, rc, rcm, s1, m1, rz, rzm, s2, m2, rx, rxm, s3, ry, full, send_sem, recv_sem):
+    at = Place()
+    at.greet()
+    sends = Sends(send_sem, recv_sem)
+    other = 1 - at.c
+    partner = at.device(c=other)
+    sends.recv([
+        sends.start(part.at[other], rc, partner),
+        sends.start(mass, rcm, partner),
+    ])
+    s1[...] = part[at.c] + rc[...]
+    m1[...] = mass[...] + rcm[...]
+
+    copies = []
+    for k, there, device in at.along("z"):
+        copies.append(sends.start(s1.at[there], rz.at[k - 1], device))
+        copies.append(sends.start(m1, rzm.at[at.z], device))
+    rzm[at.z] = m1[...]
+    sends.recv(copies)
+    s2[...] = s1[at.z] + jnp.sum(rz[...], axis=0)
+    m2[...] = jnp.sum(rzm[...], axis=0)
+
+    copies = []
+    for k, there, device in at.along("x"):
+        copies.append(sends.start(s2.at[there], rx.at[k - 1], device))
+        copies.append(sends.start(m2, rxm.at[at.x], device))
+    rxm[at.x] = m2[...]
+    sends.recv(copies)
+    s3[0] = s2[at.x] + jnp.sum(rx[...], axis=0)
+    s3[1] = jnp.sum(rxm[...], axis=0)
+
+    copies = []
+    for k, there, device in at.along("y"):
+        copies.append(sends.start(s3, ry.at[at.y], device))
+    ry[at.y] = s3[...]
+    sends.recv(copies)
+    done = jnp.sum(ry[...], axis=0)
+    mass_out[...] = done[1]
+
+    full[at.c, at.z, at.x] = done[0]
+    mine = full.at[at.c, at.z, at.x]
+    sends.recv([sends.start(mine, mine, d) for _, _, d in at.along("x")])
+    mine = full.at[at.c, at.z]
+    sends.recv([sends.start(mine, mine, d) for _, _, d in at.along("z")])
+    mine = full.at[at.c]
+    sends.recv([sends.start(mine, mine, partner)])
+    full_out[...] = full[...]
+    sends.finish()
+
+
+def total(part, mass):
+    tile = (8, 128)
+    f32 = jnp.float32
+    copies = 2 + 2 * 7 + 2 * 3 + 7 + 3 + 7 + 1
+    vmem = pl.BlockSpec(memory_space=pltpu.VMEM)
+    return pl.pallas_call(
+        total_kernel,
+        out_shape=(
+            jax.ShapeDtypeStruct((2, NZ, NX) + tile, f32),
+            jax.ShapeDtypeStruct(tile, f32),
+        ),
+        in_specs=[vmem, vmem],
+        out_specs=(vmem, vmem),
+        scratch_shapes=[
+            pltpu.VMEM((NZ, NX) + tile, f32),
+            pltpu.VMEM(tile, f32),
+            pltpu.VMEM((NZ, NX) + tile, f32),
+            pltpu.VMEM(tile, f32),
+            pltpu.VMEM((NZ - 1, NX) + tile, f32),
+            pltpu.VMEM((NZ,) + tile, f32),
+            pltpu.VMEM((NX,) + tile, f32),
+            pltpu.VMEM(tile, f32),
+            pltpu.VMEM((NX - 1,) + tile, f32),
+            pltpu.VMEM((NX,) + tile, f32),
+            pltpu.VMEM((2,) + tile, f32),
+            pltpu.VMEM((NY, 2) + tile, f32),
+            pltpu.VMEM((2, NZ, NX) + tile, f32),
+            pltpu.SemaphoreType.DMA((copies,)),
+            pltpu.SemaphoreType.DMA((copies,)),
+        ],
+        compiler_params=pltpu.CompilerParams(collective_id=1, has_side_effects=True),
+        name="total",
+    )(part, mass)
+
+
+def scatter_kernel(proj, table, proj_out, table_out, rc, rcw, s1, w1, rz, ry, rwz, a2, b2, w2, ry2, rz2, rwy, ab, w3, rx, rwx, g, send_sem, recv_sem):
+    at = Place()
+    at.greet()
+    sends = Sends(send_sem, recv_sem)
+    other = 1 - at.c
+    partner = at.device(c=other)
+    sends.recv([
+        sends.start(proj.at[:, :, other], rc, partner),
+        sends.start(table, rcw, partner),
+    ])
+    for x in range(NX):
+        for z in range(NZ):
+            columns = slice(z * 128, (z + 1) * 128)
+            s1[x, :, z] = proj[x, :, at.c, :, columns] + rc[x, :, :, columns]
+    w1[...] = table[...] + rcw[...]
+
+    copies = []
+    half = NX // 2
+    for (k, zt, zd), (_, yt, yd) in zip(at.along("z"), at.along("y")):
+        copies.append(sends.start(s1.at[pl.ds(0, half), :, zt], rz.at[k - 1], zd))
+        copies.append(sends.start(s1.at[pl.ds(half, half), yt], ry.at[k - 1], yd))
+        copies.append(sends.start(w1.at[zt], rwz.at[k - 1], zd))
+    sends.recv(copies)
+    a2[...] = s1[pl.ds(0, half), :, at.z] + jnp.sum(rz[...], axis=0)
+    b2[...] = s1[pl.ds(half, half), at.y] + jnp.sum(ry[...], axis=0)
+    w2[...] = w1[at.z] + jnp.sum(rwz[...], axis=0)
+
+    copies = []
+    for (k, zt, zd), (_, yt, yd) in zip(at.along("z"), at.along("y")):
+        copies.append(sends.start(a2.at[:, yt], ry2.at[k - 1], yd))
+        copies.append(sends.start(b2.at[:, zt], rz2.at[k - 1], zd))
+        copies.append(sends.start(w2, rwy.at[at.y], yd))
+    rwy[at.y] = w2[...]
+    sends.recv(copies)
+    ab[pl.ds(0, half)] = a2[:, at.y] + jnp.sum(ry2[...], axis=0)
+    ab[pl.ds(half, half)] = b2[:, at.z] + jnp.sum(rz2[...], axis=0)
+    w3[...] = jnp.sum(rwy[...], axis=0)
+
+    copies = []
+    for k, there, device in at.along("x"):
+        copies.append(sends.start(ab.at[there], rx.at[k - 1], device))
+        copies.append(sends.start(w3, rwx.at[at.x], device))
+    rwx[at.x] = w3[...]
+    sends.recv(copies)
+    g[at.c, at.z, 0] = ab[at.x] + jnp.sum(rx[...], axis=0)
+    g[at.c, at.z, 1] = jnp.sum(rwx[...], axis=0)
+
+    mine = g.at[at.c, at.z]
+    sends.recv([sends.start(mine, mine, d) for _, _, d in at.along("z")])
+    mine = g.at[at.c]
+    sends.recv([sends.start(mine, mine, partner)])
+    for c in range(2):
+        for z in range(NZ):
+            proj_out[c * 8 : (c + 1) * 8, z * 128 : (z + 1) * 128] = g[c, z, 0]
+    for z in range(NZ):
+        table_out[z] = g[0, z, 1]
+    sends.finish()
+
+
+def scatter(proj, table):
+    tile = (8, 128)
+    f32 = jnp.float32
+    half = NX // 2
+    copies = 2 + 3 * 7 + 3 * 7 + 2 * 3 + 7 + 1
+    vmem = pl.BlockSpec(memory_space=pltpu.VMEM)
+    return pl.pallas_call(
+        scatter_kernel,
+        out_shape=(
+            jax.ShapeDtypeStruct((16, 1024), f32),
+            jax.ShapeDtypeStruct((NZ,) + tile, f32),
+        ),
+        in_specs=[vmem, vmem],
+        out_specs=(vmem, vmem),
+        scratch_shapes=[
+            pltpu.VMEM((NX, NY, 8, 1024), f32),
+            pltpu.VMEM((NZ,) + tile, f32),
+            pltpu.VMEM((NX, NY, NZ) + tile, f32),
+            pltpu.VMEM((NZ,) + tile, f32),
+            pltpu.VMEM((NZ - 1, half, NY) + tile, f32),
+            pltpu.VMEM((NY - 1, half, NZ) + tile, f32),
+            pltpu.VMEM((NZ - 1,) + tile, f32),
+            pltpu.VMEM((half, NY) + tile, f32),
+            pltpu.VMEM((half, NZ) + tile, f32),
+            pltpu.VMEM(tile, f32),
+            pltpu.VMEM((NY - 1, half) + tile, f32),
+            pltpu.VMEM((NZ - 1, half) + tile, f32),
+            pltpu.VMEM((NY,) + tile, f32),
+            pltpu.VMEM((NX,) + tile, f32),
+            pltpu.VMEM(tile, f32),
+            pltpu.VMEM((NX - 1,) + tile, f32),
+            pltpu.VMEM((NX,) + tile, f32),
+            pltpu.VMEM((2, NZ, 2) + tile, f32),
+            pltpu.SemaphoreType.DMA((copies,)),
+            pltpu.SemaphoreType.DMA((copies,)),
+        ],
+        compiler_params=pltpu.CompilerParams(collective_id=2, has_side_effects=True),
+        name="scatter",
+    )(proj, table)
 
 
 def body(
@@ -57,19 +308,19 @@
     exp_logit = jnp.exp(partition_affinity_bound * smooth_clamping_function)
     weight = exp_logit / jnp.sum(exp_logit, axis=-1, keepdims=True)
     weight_b = weight.astype(jnp.bfloat16)
-    mass_part = jnp.sum(weight, axis=0).T
-    token_part = jnp.einsum(
-        "nhg,nhc->ghc", weight_b, feature_heads, preferred_element_type=jnp.float32
-    ).reshape(slice_count, attn_group_index * head_width)
-    back_part = jnp.einsum(
-        "nhg,nhc->ghc", weight_b, grad_heads, preferred_element_type=jnp.float32
-    ).reshape(slice_count, attn_group_index * head_width)
-    slice_mass, token_sum, back_sum = lax.psum(
-        (mass_part, token_part, back_part), ("region", "band")
-    )
-    denominator = slice_mass.T + epsilon
-    token_heads = token_sum.reshape(slice_count, attn_group_index, head_width).transpose(1, 0, 2)
-    back_heads = back_sum.reshape(slice_count, attn_group_index, head_width).transpose(1, 0, 2)
+    mass_part = jnp.sum(weight, axis=0)
+    both_heads = jnp.concatenate([feature_heads, grad_heads], axis=-1)
+    both_part = jnp.einsum(
+        "nhg,nhc->hgc", weight_b, both_heads, preferred_element_type=jnp.float32
+    )
+    full, slice_mass = total(
+        both_part.reshape(2, NZ, NX, 8, 128),
+        jnp.pad(mass_part, ((0, 0), (0, 128 - slice_count))),
+    )
+    full = full.reshape(attn_group_index, slice_count, 2 * head_width)
+    denominator = slice_mass[:, :slice_count] + epsilon
+    token_heads = full[:, :, :head_width]
+    back_heads = full[:, :, head_width:]
     tokens = token_heads / denominator[:, :, None]
     out_token, pullback = jax.vjp(token_mix, tokens, latent_query_key_value_maps)
     grad_token, grad_w_token = pullback(back_heads)
@@ -117,11 +368,11 @@
     proj_part = lax.dot_general(
         vertex_inputs, grad_joined, (((0,), (0,)), ((), ())), preferred_element_type=jnp.float32
     )
-    grad_w_slice, full_proj = lax.psum((slice_part, proj_part), ("region", "band"))
-    row_share = full_proj.shape[0] // lax.axis_size("region")
-    grad_proj = lax.dynamic_slice_in_dim(
-        full_proj, lax.axis_index("region") * row_share, row_share, 0
-    )
+    grad_proj, table = scatter(
+        proj_part.reshape(NX, NY, 2, 8, 1024),
+        jnp.pad(slice_part, ((0, 0), (0, 128 - slice_count))).reshape(NZ, 8, 128),
+    )
+    grad_w_slice = table.reshape(head_width, 128)[:, :slice_count]
     return (grad_points, grad_proj, grad_w_slice, grad_w_token)
 
 

time: 684 us -> 111 us (0.16)
  waiting for transfers between devices: 439 us -> 0 us
  blocking collectives: 205 us -> 0 us
  Pallas kernels: 0 us -> 81 us
  between operations: 14.4 us -> 0.99 us
    psum x2 -> x0, waiting for transfers between devices: 439 us -> none  [the longest x1 270 us: body(): lax.psum((slice_part, proj_part), ('region', 'band'))]
    psum x2 -> x0, blocking collectives: 205 us -> none  [the longest x1 108 us: body(): lax.psum((mass_part, token_part, back_part), ('region', 'band'))]
    pallas_call x0 -> x2, Pallas kernels: none -> 81 us  [the longest x1 43 us: total(): pl.pallas_call(total_kernel, out_shape=(jax.ShapeDtypeStruct((2, NZ, NX)...]
  transfers between devices with their start and end apart: 2 -> 0, of which waited for: 2 -> 0; matrix products, arithmetic and copies ran while one was open for 1% -> 0% of each run, Pallas kernels for 0% -> 0%
where the time goes in v1:
time: 111 us
  Pallas kernels  81 us (73%)
  matrix products  19.8 us (18%)
  local copies, waits for them, and re-layouts  6.73 us (6%)
  other arithmetic  2.31 us (2%)
    pallas_call x1, Pallas kernels, total(): pl.pallas_call(total_kernel, out_shape=(jax.ShapeDtypeStruct((2, NZ, NX)...  43 us
    pallas_call x1, Pallas kernels, scatter(): pl.pallas_call(scatter_kernel, out_shape=(jax.ShapeDtypeStruct((16, 1024)...  38 us
    unnamed x21, local copies, waits for them, and re-layouts  3.98 us
    dot_general x3, matrix products, token_mix(): jnp.einsum('hgc,cd->hgd', tokens, latent_query_key_value_maps[0], precisi...  2.52 us
    dot_general x3, matrix products, token_mix(): jnp.einsum('hgc,cd->hgd', tokens, latent_query_key_value_maps[2], precisi...  2.43 us
    dot_general x3, matrix products, token_mix(): jnp.einsum('hgc,cd->hgd', tokens, latent_query_key_value_maps[1], precisi...  2.42 us

profile of v1, /device:TPU:1, one launch (start us, length us, event | category | flops | bytes accessed | tf_op | source)
XLA Modules:
  0.0 110.8 jit_solution(9317860527689031883)
XLA Ops:
  0.7 0.8 broadcast_multiply_fusion
  1.4 1.1 copy.28
  2.5 1.2 %convolution_convert_fusion.2 = bf16[256,512]{1,0:T(8,128)(2,1)S(1)} fusion(bf16[256,512]{1,0:T(8,128)(2,1)} %param.7, bf16[512,512]{1,0:T(8,128)(2,1)S(1)} %copy-done), kind=kOutput, calls=%fused_computation.15 | convolution fusion | flops 134348800 | bytes 1048576 | tf_op jit(solution)/shard_map/dot_general | solution.py:293
  4.3 0.8 copy.25
  5.7 1.3 %fusion.25 = (f32[256,8]{0,1:T(8,128)S(1)}, f32[256,8,64]{0,2,1:T(8,128)S(1)}) fusion(f32[8]{0:T(128)S(1)} %broadcast_multiply_fusion, bf16[256,8,64]{0,2,1:T(8,128)(2,1)} %bitcast.103, bf16[64,64]{1,0:T(8,128)(2,1)S(1)} %copy-done.7), kind=kOutput, calls=%fused_computation.42 | convolution fusion | flops 17168384 | bytes 802848 | tf_op jit(solution)/shard_map/nhc,cg->nhg/dot_general | solution.py:302
  7.0 1.2 %fusion.16 = f32[8,64,128]{2,1,0:T(8,128)} fusion(bf16[256,8,64]{2,0,1:T(8,128)(2,1)S(1)} %copy.30, bf16[256,8,64]{2,0,1:T(8,128)(2,1)S(1)} %copy.29, f32[256,8,64]{0,2,1:T(8,128)S(1)} %get-tuple-element.13, f32[256,8]{0,1:T(8,128)S(1)} %get-tuple-element.12), kind=kOutput, calls=%fused_computation.31 | convolution fusion | flops 34996224 | bytes 1318912 | tf_op jit(solution)/shard_map/nhg,nhc->hgc/dot_general | solution.py:313
  9.0 43.0 %total.1 = (f32[2,8,4,8,128]{4,3,2,1,0:T(8,128)}, f32[8,128]{1,0:T(8,128)}) custom-call(f32[2,8,4,8,128]{4,3,2,1,0:T(8,128)} %bitcast.105, f32[8,128]{1,0:T(8,128)} %pad.17.mass), custom_call_target="tpu_custom_call" | custom-call | tf_op jit(solution)/shard_map/total/pallas_call | solution.py:150
  51.9 0.7 slice_add_fusion
  52.7 1.4 %fusion.44 = f32[8,64,64]{2,1,0:T(8,128)S(1)} fusion(f32[3,64,64]{2,1,0:T(8,128)S(1)} %copy-done.5, f32[8,64,128]{2,1,0:T(8,128)} %bitcast.88, f32[8,64]{1,0:T(8,128)S(1)} %slice_add_fusion), kind=kOutput, calls=%fused_computation.66 | convolution fusion | flops 25198592 | bytes 430080 | tf_op jit(solution)/shard_map/jvp(hgc,cd->hgd)/dot_general | solution.py:22
  54.1 1.4 %fusion.40 = f32[8,64,64]{2,1,0:T(8,128)S(1)} fusion(f32[3,64,64]{2,1,0:T(8,128)S(1)} %copy-done.5, f32[8,64,128]{2,1,0:T(8,128)} %bitcast.89, f32[8,64]{1,0:T(8,128)S(1)} %slice_add_fusion), kind=kOutput, calls=%fused_computation.62 | convolution fusion | flops 25198592 | bytes 430080 | tf_op jit(solution)/shard_map/jvp(hgc,cd->hgd)/dot_general | solution.py:23
  55.4 1.4 %fusion.47 = f32[8,64,64]{2,1,0:T(8,128)S(1)} fusion(f32[3,64,64]{2,1,0:T(8,128)S(1)} %copy-done.5, f32[8,64,128]{2,1,0:T(8,128)} %bitcast.90, f32[8,64]{1,0:T(8,128)S(1)} %slice_add_fusion), kind=kOutput, calls=%fused_computation.69 | convolution fusion | flops 25198592 | bytes 430080 | tf_op jit(solution)/shard_map/jvp(hgc,cd->hgd)/dot_general | solution.py:21
  57.4 0.6 fusion.11
  58.0 0.6 multiply_reduce_fusion.2
  58.7 0.7 fusion.65
  60.3 0.7 convolution_bitcast_fusion.2
  61.8 0.7 convolution_bitcast_fusion.1
  62.9 0.7 convolution_bitcast_fusion
  63.7 0.7 pad_add_fusion
  66.1 0.6 pad_bitcast_fusion.table
  67.0 1.1 fusion.8
  68.1 1.8 %fusion.20 = f32[1024,512]{0,1:T(8,128)} fusion(bf16[256,512]{1,0:T(8,128)(2,1)S(1)} %copy-done.1, bf16[256,512]{0,1:T(8,128)(2,1)S(1)} %bitcast.102, bf16[256,512]{0,1:T(8,128)(2,1)S(1)} %bitcast.100), kind=kOutput, calls=%fused_computation.35 | convolution fusion | flops 269484032 | bytes 2883584 | tf_op jit(solution)/shard_map/dot_general | solution.py:368
  69.9 38.0 %scatter.1 = (f32[16,1024]{1,0:T(8,128)}, f32[8,8,128]{2,1,0:T(8,128)}) custom-call(f32[4,8,2,8,1024]{4,3,2,1,0:T(8,128)} %bitcast.83, f32[8,8,128]{2,1,0:T(8,128)} %pad_bitcast_fusion.table), custom_call_target="tpu_custom_call" | custom-call | tf_op jit(solution)/shard_map/scatter/pallas_call | solution.py:245
  107.9 1.5 %copy.51 = f32[16,1024]{1,0:T(8,128)} copy(f32[16,1024]{1,0:T(8,128)} %get-tuple-element.25) | data formatting | bytes 131072
  109.4 1.4 %copy.52 = f32[64,64]{1,0:T(8,128)} copy(f32[64,64]{1,0:T(8,128)} %bitcast.106) | data formatting | bytes 32768
  (39 shorter events, 6.6 us)
Async XLA Ops:
  0.6 1.9 %copy-start = (bf16[512,512]{1,0:T(8,128)(2,1)S(1)}, bf16[512,512]{1,0:T(8,128)(2,1)}, u32[]{:S(2)}) copy-start(bf16[512,512]{1,0:T(8,128)(2,1)} %param.8) | copy-start | bytes 1572868
  0.6 3.3 %copy-start.1 = (bf16[256,512]{1,0:T(8,128)(2,1)S(1)}, bf16[256,512]{1,0:T(8,128)(2,1)}, u32[]{:S(2)}) copy-start(bf16[256,512]{1,0:T(8,128)(2,1)} %param.7) | copy-start | bytes 786436
  0.7 3.3 %copy-start.2 = (bf16[512,512]{1,0:T(8,128)(2,1)S(1)}, bf16[512,512]{1,0:T(8,128)(2,1)}, u32[]{:S(2)}) copy-start(bf16[512,512]{1,0:T(8,128)(2,1)} %param.9) | copy-start | bytes 1572868
  3.8 1.9 %copy-start.7 = (bf16[64,64]{1,0:T(8,128)(2,1)S(1)}, bf16[64,64]{1,0:T(8,128)(2,1)}, u32[]{:S(2)}) copy-start(bf16[64,64]{1,0:T(8,128)(2,1)} %param.10) | copy-start | bytes 24580
  7.0 45.7 %copy-start.5 = (f32[3,64,64]{2,1,0:T(8,128)S(1)}, f32[3,64,64]{2,1,0:T(8,128)}, u32[]{:S(2)}) copy-start(f32[3,64,64]{2,1,0:T(8,128)} %param.12) | copy-start | bytes 147460
  51.9 5.5 %copy-start.3 = (f32[2,8,4,8,128]{4,3,2,1,0:T(8,128)S(1)}, f32[2,8,4,8,128]{4,3,2,1,0:T(8,128)}, u32[]{:S(2)}) copy-start(f32[2,8,4,8,128]{4,3,2,1,0:T(8,128)} %get-tuple-element.8) | copy-start | bytes 786436
  61.4 2.3 %copy-start.6 = (f32[8,128]{1,0:T(8,128)S(1)}, f32[8,128]{1,0:T(8,128)}, u32[]{:S(2)}) copy-start(f32[8,128]{1,0:T(8,128)} %get-tuple-element.9) | copy-start | bytes 12292
  62.9 1.9 %copy-start.4 = (bf16[256,512]{0,1:T(8,128)(2,1)S(1)}, bf16[256,512]{0,1:T(8,128)(2,1)}, u32[]{:S(2)}) copy-start(bf16[256,512]{0,1:T(8,128)(2,1)} %copy.25) | copy-start | bytes 786436
  62.9 1.9 %copy-start.8 = (f32[8]{0:T(128)S(1)}, f32[8]{0:T(128)}, u32[]{:S(2)}) copy-start(f32[8]{0:T(128)} %param.11) | copy-start | bytes 100

commit v2 on v0

v2 whole, which is shorter than its diff:
```python
import math

import jax
import jax.numpy as jnp
from jax import lax
from jax.experimental import pallas as pl
from jax.experimental.pallas import tpu as pltpu
from jax.sharding import PartitionSpec as P

partition_affinity_bound = 8.0
score_cap = 10.0
epsilon = 1e-05

NX, NY, NZ = 4, 8, 8
MESH = pl.DeviceIdType.MESH


class Place:
    def __init__(self):
        region, band = lax.axis_index("region"), lax.axis_index("band")
        self.x, self.y = lax.div(region, NY), lax.rem(region, NY)
        self.z, self.c = lax.div(band, 2), lax.rem(band, 2)

    def device(self, x=None, y=None, z=None, c=None):
        x = self.x if x is None else x
        y = self.y if y is None else y
        z = self.z if z is None else z
        c = self.c if c is None else c
        return {"region": x * NY + y, "band": z * 2 + c}

    def along(self, axis):
        size = {"x": NX, "y": NY, "z": NZ}[axis]
        here = getattr(self, axis)
        order = sorted(range(1, size), key=lambda k: -min(k, size - k))
        for k in order:
            there = lax.rem(here + k, size)
            yield k, there, self.device(**{axis: there})

    def greet(self):
        barrier = pltpu.get_barrier_semaphore()
        count = 0
        partners = [self.device(c=1 - self.c)]
        for axis in "xyz":
            partners += [d for _, _, d in self.along(axis)]
        for d in partners:
            pl.semaphore_signal(barrier, inc=1, device_id=d, device_id_type=MESH)
            count += 1
        return lambda: pl.semaphore_wait(barrier, count)


class Sends:
    def __init__(self, send_sem, recv_sem):
        self.send_sem, self.recv_sem, self.used, self.open = send_sem, recv_sem, 0, []

    def start(self, src, dst, device):
        i = self.used
        self.used += 1
        copy = pltpu.make_async_remote_copy(
            src_ref=src,
            dst_ref=dst,
            send_sem=self.send_sem.at[i],
            recv_sem=self.recv_sem.at[i],
            device_id=device,
            device_id_type=MESH,
        )
        copy.start()
        self.open.append(copy)
        return copy

    def recv(self, copies):
        for copy in copies:
            copy.wait_recv()

    def finish(self):
        for copy in self.open:
            copy.wait_send()


HEADS, PAIRS, WIDTH = 8, 4, 64
LANES = 128
HIGHEST = lax.Precision.HIGHEST
F32, BF16 = jnp.float32, jnp.bfloat16


def dot(a, b, over=(1, 0), precision=None):
    dims = (((over[0],), (over[1],)), ((), ()))
    return lax.dot_general(a, b, dims, precision=precision, preferred_element_type=F32)


def exact(a, b, over=(1, 0)):
    return dot(a, b, over, HIGHEST)


def same_half(rows, lanes=LANES):
    r = lax.broadcasted_iota(jnp.int32, (rows, lanes), 0)
    l = lax.broadcasted_iota(jnp.int32, (rows, lanes), 1)
    return (r < WIDTH) == (l < WIDTH)


def swap(v):
    return pltpu.roll(v, WIDTH, 1)


def columns(p):
    return slice(p * LANES, (p + 1) * LANES)


def one_head(v, den, maps):
    tokens = v[:, :WIDTH] / den
    back = swap(v)[:, :WIDTH]
    q, k, w = (exact(tokens, maps[i]) for i in range(3))
    squash = jnp.tanh(exact(q, k, (1, 1)) / math.sqrt(WIDTH) / score_cap)
    e = jnp.exp(score_cap * squash)
    attention = e / jnp.sum(e, axis=1, keepdims=True)
    out = tokens + exact(attention, w)
    d_attention = exact(back, w, (1, 1))
    d_w = exact(attention, back, (0, 0))
    d_capped = attention * (
        d_attention - jnp.sum(d_attention * attention, axis=1, keepdims=True)
    )
    d_scores = d_capped * (1.0 - squash * squash) / math.sqrt(WIDTH)
    d_q = exact(d_scores, k)
    d_k = exact(d_scores, q, (0, 0))
    grad = back + exact(d_q, maps[0], (1, 1)) + exact(d_k, maps[1], (1, 1))
    grad = grad + exact(d_w, maps[2], (1, 1))
    grad_maps = [exact(tokens, d, (0, 0)) for d in (d_q, d_k, d_w)]
    grad_mass = -jnp.sum(grad * tokens, axis=1, keepdims=True) / den
    return out, grad / den, grad_mass, grad_maps


def placed(v, half):
    r = lax.broadcasted_iota(jnp.int32, (WIDTH, LANES), 0)
    l = lax.broadcasted_iota(jnp.int32, (WIDTH, LANES), 1)
    return exact(v, (l == r + half * WIDTH).astype(F32))


def kernel(
    x_ref, we_ref, ws_ref, wa_ref, sharp_ref, maps_ref, cot_ref,
    points_out, proj_out, slice_out, maps_out,
    feature, middle, weight, squash_ref, weight_b, part, mass, xt, table, gcat,
    rc, rcm, s1, m1, rz, rzm, s2, m2, rx, rxm, s3, ry, headbuf, res,
    proj, rcp, rcw, p1, w1, pz, py, wz, a2, b2, w2, py2, pz2, wy, ab, w3, px, wx, g, gt,
    send_sem, recv_sem,
):
    at = Place()
    greeted = at.greet()
    sends = Sends(send_sem, recv_sem)
    other = 1 - at.c
    partner = at.device(c=other)
    half_mask = same_half(LANES)
    ones = half_mask.astype(F32)
    lane_low = lax.broadcasted_iota(jnp.int32, (1, LANES), 1) < WIDTH

    wa = wa_ref[...]
    wa_pair = jnp.where(half_mask, wa, jnp.zeros_like(wa))

    def sharp(p):
        return jnp.where(lane_low, sharp_ref[2 * p], sharp_ref[2 * p + 1])

    feature[...] = dot(x_ref[...], we_ref[...]).astype(BF16)
    middle[...] = dot(x_ref[...], ws_ref[...]).astype(BF16)
    mass[...] = jnp.zeros_like(mass)
    for p in range(PAIRS):
        cols = columns(p)
        raw = dot(middle[:, cols], wa_pair)
        squash = jnp.tanh(raw / (partition_affinity_bound * sharp(p)))
        e = jnp.exp(partition_affinity_bound * squash)
        w = e / exact(e, ones)
        wb = w.astype(BF16)
        squash_ref[:, cols] = squash
        weight[:, cols] = w
        weight_b[:, cols] = wb
        mass[p : p + 1, :] = jnp.sum(w, axis=0, keepdims=True)
        tok = dot(wb, feature[:, cols], (0, 0))
        back = dot(wb, cot_ref[:, cols], (0, 0))
        both = jnp.where(half_mask, tok, swap(back))
        part[p // 2, 4 * (p % 2) : 4 * (p % 2) + 4] = both.reshape(4, NX, 8, LANES)

    greeted()
    copies = [
        sends.start(part.at[other], rc, partner),
        sends.start(mass, rcm, partner),
    ]
    xt[...] = x_ref[...].T
    sends.recv(copies)
    s1[...] = part[at.c] + rc[...]
    m1[...] = mass[...] + rcm[...]

    copies = []
    for k, there, device in at.along("z"):
        copies.append(sends.start(s1.at[there], rz.at[k - 1], device))
        copies.append(sends.start(m1, rzm.at[at.z], device))
    rzm[at.z] = m1[...]
    sends.recv(copies)
    s2[...] = s1[at.z] + jnp.sum(rz[...], axis=0)
    m2[...] = jnp.sum(rzm[...], axis=0)

    copies = []
    for k, there, device in at.along("x"):
        copies.append(sends.start(s2.at[there], rx.at[k - 1], device))
        copies.append(sends.start(m2, rxm.at[at.x], device))
    rxm[at.x] = m2[...]
    sends.recv(copies)
    s3[0] = s2[at.x] + jnp.sum(rx[...], axis=0)
    s3[1] = jnp.sum(rxm[...], axis=0)

    copies = []
    for k, there, device in at.along("y"):
        copies.append(sends.start(s3, ry.at[at.y], device))
    ry[at.y] = s3[...]
    sends.recv(copies)
    done = jnp.sum(ry[...], axis=0)

    zpair, zside = lax.div(at.z, 2), lax.rem(at.z, 2)
    headbuf[zside, at.x] = done[0]
    mine = headbuf.at[zside, at.x]
    sends.recv([sends.start(mine, mine, d) for _, _, d in at.along("x")])
    mine = headbuf.at[zside]
    sends.recv([sends.start(mine, mine, at.device(z=zpair * 2 + 1 - zside))])

    odd = lax.rem(zpair, 2)
    pair = at.c * 2 + lax.div(zpair, 2)
    rows8 = lax.broadcasted_iota(jnp.int32, (8, LANES), 0)
    mass_row = jnp.sum(jnp.where(rows8 == pair, done[1], 0.0), axis=0, keepdims=True)
    r = lax.broadcasted_iota(jnp.int32, (WIDTH, LANES), 0)
    l = lax.broadcasted_iota(jnp.int32, (WIDTH, LANES), 1)
    den = jnp.sum(jnp.where(l == r + odd * WIDTH, mass_row, 0.0), axis=1, keepdims=True)
    v = headbuf[...].reshape(WIDTH, LANES)
    v = jnp.where(odd == 1, swap(v), v)
    out, grad_sum, grad_mass, grad_maps = one_head(v, den + epsilon, maps_ref)
    both = placed(grad_sum, 0) + placed(out, 1)
    both = jnp.where(odd == 1, swap(both), both)
    res[at.c, zpair, :, pl.ds(0, 4)] = both.reshape(2, 4, 8, LANES)
    mass_row = jnp.sum(
        jnp.where((l == r) | (l == r + WIDTH), grad_mass, 0.0), axis=0, keepdims=True
    )
    for side in range(2):
        res[at.c, zpair, side, 4] = jnp.broadcast_to(mass_row, (8, LANES))

    mine = res.at[at.c, zpair, zside]
    copies = []
    for k in range(1, 4):
        for s in range(2):
            there = lax.rem(zpair + k, 4) * 2 + lax.rem(zside + s, 2)
            copies.append(sends.start(mine, mine, at.device(z=there)))
    scale = 1.0 / (NX * NY * 2)
    table_low = placed(grad_maps[0] * scale, 1)
    table_high = placed(grad_maps[1] * scale, 0) + placed(grad_maps[2] * scale, 1)
    sends.recv(copies)
    mine = res.at[at.c]
    sends.recv([sends.start(mine, mine, partner)])

    slice_acc = jnp.zeros((LANES, LANES), F32)
    for p in range(PAIRS):
        cols = columns(p)
        c, z0 = p // 2, (p % 2) * 2
        v = res[c, z0 : z0 + 2, :, 0:4].reshape(LANES, LANES)
        gm = jnp.where(lane_low, res[c, z0, 0, 4, 0:1], res[c, z0 + 1, 0, 4, 0:1])
        gs = jnp.where(half_mask, v, 0.0).astype(BF16)
        ob = jnp.where(half_mask, swap(v), 0.0).astype(BF16)
        gw = dot(cot_ref[:, cols], ob, (1, 1)) + dot(feature[:, cols], gs, (1, 1)) + gm
        w = weight[:, cols]
        squash = squash_ref[:, cols]
        pre = w * (gw - exact(w * gw, ones))
        gr = (pre * (1.0 - squash * squash) / sharp(p)).astype(BF16)
        gcat[p] = dot(weight_b[:, cols], gs).astype(BF16)
        gcat[PAIRS + p] = dot(gr, wa_pair, (1, 1)).astype(BF16)
        slice_acc = slice_acc + dot(middle[:, cols], gr, (0, 0))

    core_copies = []
    order = [k for k, _, _ in at.along("z")] + [0]
    for k in order:
        blk = lax.rem(at.z + k, NZ)
        r = dot(xt[...], gcat[blk]).reshape(NX, NY, 2, 8, LANES)
        for c in range(2):
            proj[c, blk] = r[:, :, c]
        core_copies.append(sends.start(proj.at[other, blk], rcp.at[blk], partner))
    sl = slice_acc[:WIDTH] + swap(slice_acc[WIDTH:])
    sl = jnp.where(lane_low, sl, 0.0)
    table[:, 0] = (sl + table_low).reshape(NZ, 8, LANES)
    table[:, 1] = table_high.reshape(NZ, 8, LANES)
    table_copy = sends.start(table, rcw, partner)

    half = NX // 2
    z_of = {k: d for k, _, d in at.along("z")}
    copies = []
    for k, copy in zip(order, core_copies):
        blk = lax.rem(at.z + k, NZ)
        copy.wait_recv()
        p1[blk] = proj[at.c, blk] + rcp[blk]
        if k:
            copies.append(sends.start(p1.at[blk, pl.ds(0, half)], pz.at[k - 1], z_of[k]))
    for k, yt, yd in at.along("y"):
        copies.append(sends.start(p1.at[:, pl.ds(half, half), yt], py.at[k - 1], yd))
    table_copy.wait_recv()
    w1[...] = table[...] + rcw[...]
    for k, zt, zd in at.along("z"):
        copies.append(sends.start(w1.at[zt], wz.at[k - 1], zd))

    points = jnp.zeros(points_out.shape, F32)
    for p in range(PAIRS):
        cols = columns(p)
        points = points + dot(gcat[p], we_ref[:, cols], (1, 1))
    for p in range(PAIRS):
        cols = columns(p)
        points = points + dot(gcat[PAIRS + p], ws_ref[:, cols], (1, 1))
    points_out[...] = points.astype(BF16)

    sends.recv(copies)
    a2[...] = p1[at.z, pl.ds(0, half)] + jnp.sum(pz[...], axis=0)
    b2[...] = p1[:, pl.ds(half, half), at.y] + jnp.sum(py[...], axis=0)
    w2[...] = w1[at.z] + jnp.sum(wz[...], axis=0)

    copies = []
    for (k, zt, zd), (_, yt, yd) in zip(at.along("z"), at.along("y")):
        copies.append(sends.start(a2.at[:, yt], py2.at[k - 1], yd))
        copies.append(sends.start(b2.at[zt], pz2.at[k - 1], zd))
        copies.append(sends.start(w2, wy.at[at.y], yd))
    wy[at.y] = w2[...]
    sends.recv(copies)
    ab[pl.ds(0, half)] = a2[:, at.y] + jnp.sum(py2[...], axis=0)
    ab[pl.ds(half, half)] = b2[at.z] + jnp.sum(pz2[...], axis=0)
    w3[...] = jnp.sum(wy[...], axis=0)

    copies = []
    for k, there, device in at.along("x"):
        copies.append(sends.start(ab.at[there], px.at[k - 1], device))
        copies.append(sends.start(w3, wx.at[at.x], device))
    wx[at.x] = w3[...]
    sends.recv(copies)
    g[at.c, at.z] = ab[at.x] + jnp.sum(px[...], axis=0)
    gt[at.z] = jnp.sum(wx[...], axis=0)

    mine, also = g.at[at.c, at.z], gt.at[at.z]
    copies = []
    for _, _, d in at.along("z"):
        copies.append(sends.start(mine, mine, d))
        copies.append(sends.start(also, also, d))
    sends.recv(copies)
    mine = g.at[at.c]
    copies = [sends.start(mine, mine, partner)]
    low = gt[:, 0].reshape(WIDTH, LANES)
    high = gt[:, 1].reshape(WIDTH, LANES)
    slice_out[...] = low[:, :WIDTH]
    maps_out[0] = swap(low)[:, :WIDTH]
    maps_out[1] = high[:, :WIDTH]
    maps_out[2] = swap(high)[:, :WIDTH]
    sends.recv(copies)
    for c in range(2):
        for z in range(NZ):
            proj_out[c * 8 : (c + 1) * 8, columns(z)] = g[c, z]
    sends.finish()


def body(
    vertex_inputs,
    partition_embed_matrix,
    selector_embed_matrix,
    partition_affinity_matrix,
    sharpness_divisor,
    latent_query_key_value_maps,
    result_cotangent,
):
    rows, width = vertex_inputs.shape
    tile = (8, LANES)
    half = NX // 2
    copies = 2 + 2 * 7 + 2 * 3 + 7 + 3 + 1 + 6 + 1 + 8 + 1 + 3 * 7 + 3 * 7 + 2 * 3 + 2 * 7 + 1
    vmem = pl.BlockSpec(memory_space=pltpu.VMEM)
    smem = pl.BlockSpec(memory_space=pltpu.SMEM)

    def f32(*shape):
        return pltpu.VMEM(shape + tile, F32)

    return pl.pallas_call(
        kernel,
        out_shape=(
            jax.ShapeDtypeStruct((rows, width), BF16),
            jax.ShapeDtypeStruct((16, 1024), F32),
            jax.ShapeDtypeStruct((WIDTH, WIDTH), F32),
            jax.ShapeDtypeStruct((3, WIDTH, WIDTH), F32),
        ),
        in_specs=[vmem, vmem, vmem, vmem, smem, vmem, vmem],
        out_specs=(vmem, vmem, vmem, vmem),
        scratch_shapes=[
            pltpu.VMEM((rows, width), BF16),
            pltpu.VMEM((rows, width), BF16),
            pltpu.VMEM((rows, width), F32),
            pltpu.VMEM((rows, width), F32),
            pltpu.VMEM((rows, width), BF16),
            f32(2, NZ, NX),
            f32(),
            pltpu.VMEM((width, rows), BF16),
            f32(NZ, 2),
            pltpu.VMEM((NZ, rows, LANES), BF16),
            f32(NZ, NX),
            f32(),
            f32(NZ, NX),
            f32(),
            f32(NZ - 1, NX),
            f32(NZ),
            f32(NX),
            f32(),
            f32(NX - 1),
            f32(NX),
            f32(2),
            f32(NY, 2),
            f32(2, NX),
            f32(2, 4, 2, 5),
            f32(2, NZ, NX, NY),
            f32(NZ, NX, NY),
            f32(NZ, 2),
            f32(NZ, NX, NY),
            f32(NZ, 2),
            f32(NZ - 1, half, NY),
            f32(NY - 1, NZ, half),
            f32(NZ - 1, 2),
            f32(half, NY),
            f32(NZ, half),
            f32(2),
            f32(NY - 1, half),
            f32(NZ - 1, half),
            f32(NY, 2),
            f32(NX),
            f32(2),
            f32(NX - 1),
            f32(NX, 2),
            f32(2, NZ),
            f32(NZ, 2),
            pltpu.SemaphoreType.DMA((copies,)),
            pltpu.SemaphoreType.DMA((copies,)),
        ],
        compiler_params=pltpu.CompilerParams(collective_id=1, has_side_effects=True),
        name="layer",
    )(
        vertex_inputs,
        partition_embed_matrix,
        selector_embed_matrix,
        jnp.tile(partition_affinity_matrix, (2, 2)),
        sharpness_divisor,
        latent_query_key_value_maps,
        result_cotangent,
    )


def solution(mesh):
    return jax.shard_map(
        body,
        mesh=mesh,
        in_specs=(
            P(("region", "band"), None),
            P(),
            P(),
            P(),
            P(),
            P(),
            P(("region", "band"), None),
        ),
        out_specs=(P(("region", "band"), None), P("region", None), P(), P()),
        check_vma=False,
    )
```

time: 684 us -> 90.2 us (0.13)
  waiting for transfers between devices: 439 us -> 0 us
  blocking collectives: 205 us -> 0 us
  Pallas kernels: 0 us -> 84.1 us
  matrix products: 20.3 us -> 0 us
  between operations: 14.4 us -> 0.65 us
    psum x2 -> x0, waiting for transfers between devices: 439 us -> none  [the longest x1 270 us: body(): lax.psum((slice_part, proj_part), ('region', 'band'))]
    psum x2 -> x0, blocking collectives: 205 us -> none  [the longest x1 108 us: body(): lax.psum((mass_part, token_part, back_part), ('region', 'band'))]
    pallas_call x0 -> x1, Pallas kernels: none -> 84.1 us  [body(): pl.pallas_call(kernel, out_shape=(jax.ShapeDtypeStruct((rows, width), BF1...]
    dot_general x28 -> x0, matrix products: 20.3 us -> none  [the longest x3 2.51 us: token_mix(): jnp.einsum('hgc,cd->hgd', tokens, latent_query_key_value_maps[0], precisi...]
  transfers between devices with their start and end apart: 2 -> 0, of which waited for: 2 -> 0; matrix products, arithmetic and copies ran while one was open for 1% -> 0% of each run, Pallas kernels for 0% -> 0%
where the time goes in v2:
time: 90.2 us; the launch traced here: 89.9 us
  Pallas kernels  84.1 us (93%)
  local copies, waits for them, and re-layouts  5.19 us (6%)
    pallas_call x1, Pallas kernels, body(): pl.pallas_call(kernel, out_shape=(jax.ShapeDtypeStruct((rows, width), BF1...  84.1 us
    unnamed x10, local copies, waits for them, and re-layouts  3.72 us

profile of v2, /device:TPU:1, one launch (start us, length us, event | category | flops | bytes accessed | tf_op | source)
XLA Modules:
  0.0 89.9 jit_solution(1390077334300791706)
XLA Ops:
  0.6 0.8 tile.4
  1.4 0.7 tile.10.wa_ref
  2.1 84.1 %layer.1 = (bf16[256,512]{1,0:T(8,128)(2,1)}, f32[16,1024]{1,0:T(8,128)}, f32[64,64]{1,0:T(8,128)}, f32[3,64,64]{2,1,0:T(8,128)}) custom-call(bf16[256,512]{1,0:T(8,128)(2,1)} %x_ref.1, bf16[512,512]{1,0:T(8,128)(2,1)} %we_ref.1, bf16[512,512]{1,0:T(8,128)(2,1)} %ws_ref.1, bf16[128,128]{1,0:T(8,128)(2,1)} %tile.10.wa_ref, f32[8]{0:T(128)} %sharp_ref.1, ...), custom_call_target="tpu_custom_call" | custom-call | tf_op jit(solution)/shard_map/layer/pallas_call | solution.py:374
  86.2 0.0 copy-start.1
  86.2 1.7 %copy.15 = bf16[256,512]{1,0:T(8,128)(2,1)} copy(bf16[256,512]{1,0:T(8,128)(2,1)} %get-tuple-element.8) | data formatting | bytes 524288
  87.9 0.0 copy-done.1
  87.9 0.0 copy-start.2
  87.9 0.0 copy-start
  87.9 0.6 copy.16
  88.6 0.1 copy-done.2
  88.7 0.6 copy.17
  89.3 0.0 copy-done
  89.3 0.6 copy.18
Async XLA Ops:
  86.2 1.7 %copy-start.1 = (f32[16,1024]{1,0:T(8,128)S(1)}, f32[16,1024]{1,0:T(8,128)}, u32[]{:S(2)}) copy-start(f32[16,1024]{1,0:T(8,128)} %get-tuple-element.9) | copy-start | bytes 196612
  87.9 0.8 copy-start.2
  87.9 1.4 %copy-start = (f32[3,64,64]{2,1,0:T(8,128)S(1)}, f32[3,64,64]{2,1,0:T(8,128)}, u32[]{:S(2)}) copy-start(f32[3,64,64]{2,1,0:T(8,128)} %get-tuple-element.11) | copy-start | bytes 147460

commit v3 on v2

--- a/solution.py
+++ b/solution.py
@@ -151,8 +151,11 @@
     ones = half_mask.astype(F32)
     lane_low = lax.broadcasted_iota(jnp.int32, (1, LANES), 1) < WIDTH
 
-    wa = wa_ref[...]
-    wa_pair = jnp.where(half_mask, wa, jnp.zeros_like(wa))
+    r = lax.broadcasted_iota(jnp.int32, (LANES, WIDTH), 0)
+    l = lax.broadcasted_iota(jnp.int32, (LANES, WIDTH), 1)
+    twice = ((l == r) | (l == r - WIDTH)).astype(BF16)
+    wa_pair = dot(dot(twice, wa_ref[...]).astype(BF16), twice, (1, 1))
+    wa_pair = jnp.where(half_mask, wa_pair, 0.0).astype(BF16)
 
     def sharp(p):
         return jnp.where(lane_low, sharp_ref[2 * p], sharp_ref[2 * p + 1])
@@ -174,7 +177,7 @@
         tok = dot(wb, feature[:, cols], (0, 0))
         back = dot(wb, cot_ref[:, cols], (0, 0))
         both = jnp.where(half_mask, tok, swap(back))
-        part[p // 2, 4 * (p % 2) : 4 * (p % 2) + 4] = both.reshape(4, NX, 8, LANES)
+        part[p // 2, 2 * (p % 2) : 2 * (p % 2) + 2] = both.reshape(2, NZ, 8, LANES)
 
     greeted()
     copies = [
@@ -187,22 +190,22 @@
     m1[...] = mass[...] + rcm[...]
 
     copies = []
+    for k, there, device in at.along("x"):
+        copies.append(sends.start(s1.at[there], rx.at[k - 1], device))
+        copies.append(sends.start(m1, rxm.at[at.x], device))
+    rxm[at.x] = m1[...]
+    sends.recv(copies)
+    s2[...] = s1[at.x] + jnp.sum(rx[...], axis=0)
+    m2[...] = jnp.sum(rxm[...], axis=0)
+
+    copies = []
     for k, there, device in at.along("z"):
-        copies.append(sends.start(s1.at[there], rz.at[k - 1], device))
-        copies.append(sends.start(m1, rzm.at[at.z], device))
-    rzm[at.z] = m1[...]
-    sends.recv(copies)
-    s2[...] = s1[at.z] + jnp.sum(rz[...], axis=0)
-    m2[...] = jnp.sum(rzm[...], axis=0)
-
-    copies = []
-    for k, there, device in at.along("x"):
-        copies.append(sends.start(s2.at[there], rx.at[k - 1], device))
-        copies.append(sends.start(m2, rxm.at[at.x], device))
-    rxm[at.x] = m2[...]
-    sends.recv(copies)
-    s3[0] = s2[at.x] + jnp.sum(rx[...], axis=0)
-    s3[1] = jnp.sum(rxm[...], axis=0)
+        copies.append(sends.start(s2.at[there], rz.at[k - 1], device))
+        copies.append(sends.start(m2, rzm.at[at.z], device))
+    rzm[at.z] = m2[...]
+    sends.recv(copies)
+    s3[0] = s2[at.z] + jnp.sum(rz[...], axis=0)
+    s3[1] = jnp.sum(rzm[...], axis=0)
 
     copies = []
     for k, there, device in at.along("y"):
@@ -211,15 +214,12 @@
     sends.recv(copies)
     done = jnp.sum(ry[...], axis=0)
 
-    zpair, zside = lax.div(at.z, 2), lax.rem(at.z, 2)
-    headbuf[zside, at.x] = done[0]
-    mine = headbuf.at[zside, at.x]
-    sends.recv([sends.start(mine, mine, d) for _, _, d in at.along("x")])
-    mine = headbuf.at[zside]
-    sends.recv([sends.start(mine, mine, at.device(z=zpair * 2 + 1 - zside))])
-
-    odd = lax.rem(zpair, 2)
-    pair = at.c * 2 + lax.div(zpair, 2)
+    headbuf[at.z] = done[0]
+    mine = headbuf.at[at.z]
+    sends.recv([sends.start(mine, mine, d) for _, _, d in at.along("z")])
+
+    odd = lax.rem(at.x, 2)
+    pair = at.c * 2 + lax.div(at.x, 2)
     rows8 = lax.broadcasted_iota(jnp.int32, (8, LANES), 0)
     mass_row = jnp.sum(jnp.where(rows8 == pair, done[1], 0.0), axis=0, keepdims=True)
     r = lax.broadcasted_iota(jnp.int32, (WIDTH, LANES), 0)
@@ -230,32 +230,30 @@
     out, grad_sum, grad_mass, grad_maps = one_head(v, den + epsilon, maps_ref)
     both = placed(grad_sum, 0) + placed(out, 1)
     both = jnp.where(odd == 1, swap(both), both)
-    res[at.c, zpair, :, pl.ds(0, 4)] = both.reshape(2, 4, 8, LANES)
+    res[at.c, at.x, pl.ds(0, NZ)] = both.reshape(NZ, 8, LANES)
     mass_row = jnp.sum(
         jnp.where((l == r) | (l == r + WIDTH), grad_mass, 0.0), axis=0, keepdims=True
     )
-    for side in range(2):
-        res[at.c, zpair, side, 4] = jnp.broadcast_to(mass_row, (8, LANES))
-
-    mine = res.at[at.c, zpair, zside]
-    copies = []
-    for k in range(1, 4):
-        for s in range(2):
-            there = lax.rem(zpair + k, 4) * 2 + lax.rem(zside + s, 2)
-            copies.append(sends.start(mine, mine, at.device(z=there)))
-    scale = 1.0 / (NX * NY * 2)
+    res[at.c, at.x, NZ] = jnp.broadcast_to(mass_row, (8, LANES))
+
+    mine = res.at[at.c, at.x]
+    copies = [(k, sends.start(mine, mine, d)) for k, _, d in at.along("x")]
+    passed = [sends.start(mine, mine, partner)]
+    scale = 1.0 / (NY * NZ)
     table_low = placed(grad_maps[0] * scale, 1)
     table_high = placed(grad_maps[1] * scale, 0) + placed(grad_maps[2] * scale, 1)
-    sends.recv(copies)
-    mine = res.at[at.c]
-    sends.recv([sends.start(mine, mine, partner)])
+    for k, copy in copies:
+        copy.wait_recv()
+        came = res.at[at.c, lax.rem(at.x + NX - k, NX)]
+        passed.append(sends.start(came, came, partner))
+    sends.recv(passed)
 
     slice_acc = jnp.zeros((LANES, LANES), F32)
     for p in range(PAIRS):
         cols = columns(p)
-        c, z0 = p // 2, (p % 2) * 2
-        v = res[c, z0 : z0 + 2, :, 0:4].reshape(LANES, LANES)
-        gm = jnp.where(lane_low, res[c, z0, 0, 4, 0:1], res[c, z0 + 1, 0, 4, 0:1])
+        c, x0 = p // 2, (p % 2) * 2
+        v = res[c, x0 : x0 + 2, 0:NZ].reshape(LANES, LANES)
+        gm = jnp.where(lane_low, res[c, x0, NZ, 0:1], res[c, x0 + 1, NZ, 0:1])
         gs = jnp.where(half_mask, v, 0.0).astype(BF16)
         ob = jnp.where(half_mask, swap(v), 0.0).astype(BF16)
         gw = dot(cot_ref[:, cols], ob, (1, 1)) + dot(feature[:, cols], gs, (1, 1)) + gm
@@ -290,8 +288,8 @@
         p1[blk] = proj[at.c, blk] + rcp[blk]
         if k:
             copies.append(sends.start(p1.at[blk, pl.ds(0, half)], pz.at[k - 1], z_of[k]))
-    for k, yt, yd in at.along("y"):
-        copies.append(sends.start(p1.at[:, pl.ds(half, half), yt], py.at[k - 1], yd))
+        for j, yt, yd in at.along("y"):
+            copies.append(sends.start(p1.at[blk, pl.ds(half, half), yt], py.at[j - 1, blk], yd))
     table_copy.wait_recv()
     w1[...] = table[...] + rcw[...]
     for k, zt, zd in at.along("z"):
@@ -350,6 +348,15 @@
         for z in range(NZ):
             proj_out[c * 8 : (c + 1) * 8, columns(z)] = g[c, z]
     sends.finish()
+
+
+def store_kernel(*refs):
+    sem = refs[8]
+    copies = [pltpu.make_async_copy(refs[i], refs[4 + i], sem.at[i]) for i in range(4)]
+    for copy in copies:
+        copy.start()
+    for copy in copies:
+        copy.wait()
 
 
 def body(
@@ -364,14 +371,14 @@
     rows, width = vertex_inputs.shape
     tile = (8, LANES)
     half = NX // 2
-    copies = 2 + 2 * 7 + 2 * 3 + 7 + 3 + 1 + 6 + 1 + 8 + 1 + 3 * 7 + 3 * 7 + 2 * 3 + 2 * 7 + 1
+    copies = 2 + 2 * 3 + 2 * 7 + 7 + 7 + 3 + 4 + 8 + 1 + 7 + 8 * 7 + 7 + 3 * 7 + 2 * 3 + 2 * 7 + 1
     vmem = pl.BlockSpec(memory_space=pltpu.VMEM)
     smem = pl.BlockSpec(memory_space=pltpu.SMEM)
 
     def f32(*shape):
         return pltpu.VMEM(shape + tile, F32)
 
-    return pl.pallas_call(
+    results = pl.pallas_call(
         kernel,
         out_shape=(
             jax.ShapeDtypeStruct((rows, width), BF16),
@@ -387,25 +394,25 @@
             pltpu.VMEM((rows, width), F32),
             pltpu.VMEM((rows, width), F32),
             pltpu.VMEM((rows, width), BF16),
-            f32(2, NZ, NX),
+            f32(2, NX, NZ),
             f32(),
             pltpu.VMEM((width, rows), BF16),
             f32(NZ, 2),
             pltpu.VMEM((NZ, rows, LANES), BF16),
-            f32(NZ, NX),
+            f32(NX, NZ),
             f32(),
-            f32(NZ, NX),
+            f32(NX, NZ),
             f32(),
-            f32(NZ - 1, NX),
+            f32(NZ - 1),
             f32(NZ),
-            f32(NX),
+            f32(NZ),
             f32(),
-            f32(NX - 1),
+            f32(NX - 1, NZ),
             f32(NX),
             f32(2),
             f32(NY, 2),
-            f32(2, NX),
-            f32(2, 4, 2, 5),
+            f32(NZ),
+            f32(2, NX, NZ + 1),
             f32(2, NZ, NX, NY),
             f32(NZ, NX, NY),
             f32(NZ, 2),
@@ -435,11 +442,19 @@
         vertex_inputs,
         partition_embed_matrix,
         selector_embed_matrix,
-        jnp.tile(partition_affinity_matrix, (2, 2)),
+        partition_affinity_matrix,
         sharpness_divisor,
         latent_query_key_value_maps,
         result_cotangent,
     )
+    return pl.pallas_call(
+        store_kernel,
+        out_shape=tuple(jax.ShapeDtypeStruct(r.shape, r.dtype) for r in results),
+        in_specs=[vmem] * 4,
+        out_specs=(pl.BlockSpec(memory_space=pl.ANY),) * 4,
+        scratch_shapes=[pltpu.SemaphoreType.DMA((4,))],
+        name="store",
+    )(*results)
 
 
 def solution(mesh):

time: 90.2 us -> 84.2 us (0.933)
  local copies, waits for them, and re-layouts: 5.19 us -> 0 us
    unnamed x10 -> x0, local copies, waits for them, and re-layouts: 3.72 us -> none
    pallas_call x1, Pallas kernels: 84.1 us -> 81.6 us  [body(): pl.pallas_call(kernel, out_shape=(jax.ShapeDtypeStruct((rows, width), BF1...]
    pallas_call x0 -> x1, Pallas kernels: none -> 1.82 us  [body(): pl.pallas_call(store_kernel, out_shape=tuple((jax.ShapeDtypeStruct(r.shap...]
    another operation x2 -> x0, local copies, waits for them, and re-layouts: 1.47 us -> none  [body(): jnp.tile(partition_affinity_matrix, (2, 2))]
where the time goes in v3:
time: 84.2 us; the launch traced here: 84 us
  Pallas kernels  83.4 us (99%)
    pallas_call x1, Pallas kernels, body(): pl.pallas_call(kernel, out_shape=(jax.ShapeDtypeStruct((rows, width), BF1...  81.6 us
    pallas_call x1, Pallas kernels, body(): pl.pallas_call(store_kernel, out_shape=tuple((jax.ShapeDtypeStruct(r.shap...  1.82 us

profile of v3, /device:TPU:1, one launch (start us, length us, event | category | flops | bytes accessed | tf_op | source)
XLA Modules:
  0.0 84.0 jit_solution(5013922014578373143)
XLA Ops:
  0.6 81.6 %layer.1 = (bf16[256,512]{1,0:T(8,128)(2,1)}, f32[16,1024]{1,0:T(8,128)}, f32[64,64]{1,0:T(8,128)}, f32[3,64,64]{2,1,0:T(8,128)}) custom-call(bf16[256,512]{1,0:T(8,128)(2,1)} %x_ref.1, bf16[512,512]{1,0:T(8,128)(2,1)} %we_ref.1, bf16[512,512]{1,0:T(8,128)(2,1)} %ws_ref.1, bf16[64,64]{1,0:T(8,128)(2,1)} %wa_ref.1, f32[8]{0:T(128)} %sharp_ref.1, ...), custom_call_target="tpu_custom_call" | custom-call | tf_op jit(solution)/shard_map/layer/pallas_call | solution.py:381
  82.2 1.8 %store.1 = (bf16[256,512]{1,0:T(8,128)(2,1)}, f32[16,1024]{1,0:T(8,128)}, f32[64,64]{1,0:T(8,128)}, f32[3,64,64]{2,1,0:T(8,128)}) custom-call(bf16[256,512]{1,0:T(8,128)(2,1)} %get-tuple-element.8.refs_0_, f32[16,1024]{1,0:T(8,128)} %get-tuple-element.9.refs_1_, f32[64,64]{1,0:T(8,128)} %get-tuple-element.10.refs_2_, f32[3,64,64]{2,1,0:T(8,128)} %get-tuple-element.11.refs_3_), custom_call_target="tpu_custom_call" | custom-call | tf_op jit(solution)/shard_map/store/pallas_call | solution.py:450

commit v4 on v3

--- a/solution.py
+++ b/solution.py
@@ -52,10 +52,10 @@
     def __init__(self, send_sem, recv_sem):
         self.send_sem, self.recv_sem, self.used, self.open = send_sem, recv_sem, 0, []
 
-    def start(self, src, dst, device):
+    def plan(self, src, dst, device):
         i = self.used
         self.used += 1
-        copy = pltpu.make_async_remote_copy(
+        return pltpu.make_async_remote_copy(
             src_ref=src,
             dst_ref=dst,
             send_sem=self.send_sem.at[i],
@@ -63,6 +63,9 @@
             device_id=device,
             device_id_type=MESH,
         )
+
+    def start(self, src, dst, device):
+        copy = self.plan(src, dst, device)
         copy.start()
         self.open.append(copy)
         return copy
@@ -140,6 +143,7 @@
     feature, middle, weight, squash_ref, weight_b, part, mass, xt, table, gcat,
     rc, rcm, s1, m1, rz, rzm, s2, m2, rx, rxm, s3, ry, headbuf, res,
     proj, rcp, rcw, p1, w1, pz, py, wz, a2, b2, w2, py2, pz2, wy, ab, w3, px, wx, g, gt,
+    pxc, c2, pzc, c3, pyc,
     send_sem, recv_sem,
 ):
     at = Place()
@@ -269,9 +273,10 @@
     order = [k for k, _, _ in at.along("z")] + [0]
     for k in order:
         blk = lax.rem(at.z + k, NZ)
-        r = dot(xt[...], gcat[blk]).reshape(NX, NY, 2, 8, LANES)
+        r = dot(xt[...], gcat[blk]).reshape(NX, NY // 2, 2, 2, 8, LANES)
         for c in range(2):
-            proj[c, blk] = r[:, :, c]
+            for side in range(2):
+                proj[c, blk, side] = r[:, :, side, c]
         core_copies.append(sends.start(proj.at[other, blk], rcp.at[blk], partner))
     sl = slice_acc[:WIDTH] + swap(slice_acc[WIDTH:])
     sl = jnp.where(lane_low, sl, 0.0)
@@ -280,16 +285,40 @@
     table_copy = sends.start(table, rcw, partner)
 
     half = NX // 2
+    y_odd = lax.rem(at.y, 2) == 1
+    y_even = lax.rem(at.y, 2) == 0
+    yh = lax.div(at.y, 2)
+    owed = []
+
+    def to_side(side, src, dst):
+        planned = [(j, sends.plan(src(j, yt), dst(j), yd)) for j, yt, yd in at.along("y")]
+        for mine, cond in ((1, y_odd), (0, y_even)):
+            group = [copy for j, copy in planned if (j + mine) % 2 == side]
+            owed.append((cond, group))
+
+            @pl.when(cond)
+            def _():
+                for copy in group:
+                    copy.start()
+
+        return [copy for _, copy in planned]
+
+    c_copies, b_copies = [], []
     z_of = {k: d for k, _, d in at.along("z")}
     copies = []
     for k, copy in zip(order, core_copies):
         blk = lax.rem(at.z + k, NZ)
         copy.wait_recv()
         p1[blk] = proj[at.c, blk] + rcp[blk]
+        for j, xt_, xd in at.along("x"):
+            c_copies.append(sends.start(p1.at[blk, 0, xt_], pxc.at[j - 1, blk], xd))
         if k:
-            copies.append(sends.start(p1.at[blk, pl.ds(0, half)], pz.at[k - 1], z_of[k]))
-        for j, yt, yd in at.along("y"):
-            copies.append(sends.start(p1.at[blk, pl.ds(half, half), yt], py.at[j - 1, blk], yd))
+            copies.append(sends.start(p1.at[blk, 1, pl.ds(0, half)], pz.at[k - 1], z_of[k]))
+        b_copies += to_side(
+            1,
+            lambda j, yt: p1.at[blk, 1, pl.ds(half, half), lax.div(yt, 2)],
+            lambda j: py.at[j - 1, blk],
+        )
     table_copy.wait_recv()
     w1[...] = table[...] + rcw[...]
     for k, zt, zd in at.along("z"):
@@ -304,29 +333,55 @@
         points = points + dot(gcat[PAIRS + p], ws_ref[:, cols], (1, 1))
     points_out[...] = points.astype(BF16)
 
-    sends.recv(copies)
-    a2[...] = p1[at.z, pl.ds(0, half)] + jnp.sum(pz[...], axis=0)
-    b2[...] = p1[:, pl.ds(half, half), at.y] + jnp.sum(py[...], axis=0)
+    sends.recv(c_copies)
+    c2[...] = p1[:, 0, at.x] + jnp.sum(pxc[...], axis=0)
+    c_copies = [sends.start(c2.at[zt], pzc.at[k - 1], zd) for k, zt, zd in at.along("z")]
+
+    sends.recv(copies)
+    a2[...] = p1[at.z, 1, pl.ds(0, half)] + jnp.sum(pz[...], axis=0)
+    a_copies = to_side(1, lambda j, yt: a2.at[:, lax.div(yt, 2)], lambda j: py2.at[j - 1])
     w2[...] = w1[at.z] + jnp.sum(wz[...], axis=0)
-
-    copies = []
-    for (k, zt, zd), (_, yt, yd) in zip(at.along("z"), at.along("y")):
-        copies.append(sends.start(a2.at[:, yt], py2.at[k - 1], yd))
-        copies.append(sends.start(b2.at[zt], pz2.at[k - 1], zd))
-        copies.append(sends.start(w2, wy.at[at.y], yd))
+    copies = [sends.start(w2, wy.at[at.y], yd) for _, _, yd in at.along("y")]
     wy[at.y] = w2[...]
-    sends.recv(copies)
-    ab[pl.ds(0, half)] = a2[:, at.y] + jnp.sum(py2[...], axis=0)
-    ab[pl.ds(half, half)] = b2[at.z] + jnp.sum(pz2[...], axis=0)
+    b_next = [sends.plan(b2.at[zt], pz2.at[k - 1], zd) for k, zt, zd in at.along("z")]
+
+    @pl.when(y_odd)
+    def _():
+        sends.recv(b_copies)
+        b2[...] = p1[:, 1, pl.ds(half, half), yh] + jnp.sum(py[...], axis=0)
+        for copy in b_next:
+            copy.start()
+
+    owed.append((y_odd, b_next))
+
+    sends.recv(c_copies)
+    c3[...] = c2[at.z] + jnp.sum(pzc[...], axis=0)
+    c_copies = to_side(0, lambda j, yt: c3.at[lax.div(yt, 2)], lambda j: pyc.at[j - 1])
+
+    sends.recv(copies)
     w3[...] = jnp.sum(wy[...], axis=0)
-
-    copies = []
-    for k, there, device in at.along("x"):
-        copies.append(sends.start(ab.at[there], px.at[k - 1], device))
-        copies.append(sends.start(w3, wx.at[at.x], device))
+    copies = [sends.start(w3, wx.at[at.x], xd) for _, _, xd in at.along("x")]
     wx[at.x] = w3[...]
-    sends.recv(copies)
-    g[at.c, at.z] = ab[at.x] + jnp.sum(px[...], axis=0)
+    ab_next = [sends.plan(ab.at[there], px.at[k - 1], xd) for k, there, xd in at.along("x")]
+    owed.append((y_odd, ab_next))
+
+    @pl.when(y_odd)
+    def _():
+        sends.recv(a_copies)
+        sends.recv(b_next)
+        ab[pl.ds(0, half)] = a2[:, yh] + jnp.sum(py2[...], axis=0)
+        ab[pl.ds(half, half)] = b2[at.z] + jnp.sum(pz2[...], axis=0)
+        for copy in ab_next:
+            copy.start()
+        sends.recv(ab_next)
+        g[at.c, at.z] = ab[at.x] + jnp.sum(px[...], axis=0)
+
+    @pl.when(y_even)
+    def _():
+        sends.recv(c_copies)
+        g[at.c, at.z] = c3[yh] + jnp.sum(pyc[...], axis=0)
+
+    sends.recv(copies)
     gt[at.z] = jnp.sum(wx[...], axis=0)
 
     mine, also = g.at[at.c, at.z], gt.at[at.z]
@@ -348,6 +403,12 @@
         for z in range(NZ):
             proj_out[c * 8 : (c + 1) * 8, columns(z)] = g[c, z]
     sends.finish()
+    for cond, group in owed:
+
+        @pl.when(cond)
+        def _():
+            for copy in group:
+                copy.wait_send()
 
 
 def store_kernel(*refs):
@@ -370,8 +431,9 @@
 ):
     rows, width = vertex_inputs.shape
     tile = (8, LANES)
-    half = NX // 2
-    copies = 2 + 2 * 3 + 2 * 7 + 7 + 7 + 3 + 4 + 8 + 1 + 7 + 8 * 7 + 7 + 3 * 7 + 2 * 3 + 2 * 7 + 1
+    half, yside = NX // 2, NY // 2
+    copies = 2 + 2 * 3 + 2 * 7 + 7 + 7 + 3 + 4 + 8 + 1 + 8 * 3 + 7 + 8 * 7 + 7
+    copies += 4 * 7 + 3 + 3 + 7 + 2 * 7 + 1
     vmem = pl.BlockSpec(memory_space=pltpu.VMEM)
     smem = pl.BlockSpec(memory_space=pltpu.SMEM)
 
@@ -413,15 +475,15 @@
             f32(NY, 2),
             f32(NZ),
             f32(2, NX, NZ + 1),
-            f32(2, NZ, NX, NY),
-            f32(NZ, NX, NY),
+            f32(2, NZ, 2, NX, yside),
+            f32(NZ, 2, NX, yside),
             f32(NZ, 2),
-            f32(NZ, NX, NY),
+            f32(NZ, 2, NX, yside),
             f32(NZ, 2),
-            f32(NZ - 1, half, NY),
+            f32(NZ - 1, half, yside),
             f32(NY - 1, NZ, half),
             f32(NZ - 1, 2),
-            f32(half, NY),
+            f32(half, yside),
             f32(NZ, half),
             f32(2),
             f32(NY - 1, half),
@@ -433,6 +495,11 @@
             f32(NX, 2),
             f32(2, NZ),
             f32(NZ, 2),
+            f32(NX - 1, NZ, yside),
+            f32(NZ, yside),
+            f32(NZ - 1, yside),
+            f32(yside),
+            f32(NY - 1),
             pltpu.SemaphoreType.DMA((copies,)),
             pltpu.SemaphoreType.DMA((copies,)),
         ],

time: 84.2 us -> 78.6 us (0.933)
  Pallas kernels: 83.4 us -> 77.8 us
    pallas_call x1, Pallas kernels: 81.6 us -> 75.9 us  [body(): pl.pallas_call(kernel, out_shape=(jax.ShapeDtypeStruct((rows, width), BF1...]
where the time goes in v4:
time: 78.6 us; the launch traced here: 78.4 us
  Pallas kernels  77.8 us (99%)
    pallas_call x1, Pallas kernels, body(): pl.pallas_call(kernel, out_shape=(jax.ShapeDtypeStruct((rows, width), BF1...  75.9 us
    pallas_call x1, Pallas kernels, body(): pl.pallas_call(store_kernel, out_shape=tuple((jax.ShapeDtypeStruct(r.shap...  1.82 us

profile of v4, /device:TPU:1, one launch (start us, length us, event | category | flops | bytes accessed | tf_op | source)
XLA Modules:
  0.0 78.4 jit_solution(10947743567597618494)
XLA Ops:
  0.6 75.9 %layer.1 = (bf16[256,512]{1,0:T(8,128)(2,1)}, f32[16,1024]{1,0:T(8,128)}, f32[64,64]{1,0:T(8,128)}, f32[3,64,64]{2,1,0:T(8,128)}) custom-call(bf16[256,512]{1,0:T(8,128)(2,1)} %x_ref.1, bf16[512,512]{1,0:T(8,128)(2,1)} %we_ref.1, bf16[512,512]{1,0:T(8,128)(2,1)} %ws_ref.1, bf16[64,64]{1,0:T(8,128)(2,1)} %wa_ref.1, f32[8]{0:T(128)} %sharp_ref.1, ...), custom_call_target="tpu_custom_call" | custom-call | tf_op jit(solution)/shard_map/layer/pallas_call | solution.py:443
  76.6 1.8 %store.1 = (bf16[256,512]{1,0:T(8,128)(2,1)}, f32[16,1024]{1,0:T(8,128)}, f32[64,64]{1,0:T(8,128)}, f32[3,64,64]{2,1,0:T(8,128)}) custom-call(bf16[256,512]{1,0:T(8,128)(2,1)} %get-tuple-element.8.refs_0_, f32[16,1024]{1,0:T(8,128)} %get-tuple-element.9.refs_1_, f32[64,64]{1,0:T(8,128)} %get-tuple-element.10.refs_2_, f32[3,64,64]{2,1,0:T(8,128)} %get-tuple-element.11.refs_3_), custom_call_target="tpu_custom_call" | custom-call | tf_op jit(solution)/shard_map/store/pallas_call | solution.py:517

commit v5 on v4

--- a/solution.py
+++ b/solution.py
@@ -167,8 +167,10 @@
     feature[...] = dot(x_ref[...], we_ref[...]).astype(BF16)
     middle[...] = dot(x_ref[...], ws_ref[...]).astype(BF16)
     mass[...] = jnp.zeros_like(mass)
-    for p in range(PAIRS):
-        cols = columns(p)
+    for i in range(PAIRS):
+        core = other if i < 2 else at.c
+        p = core * 2 + i % 2
+        cols = pl.ds(pl.multiple_of(p * LANES, LANES), LANES)
         raw = dot(middle[:, cols], wa_pair)
         squash = jnp.tanh(raw / (partition_affinity_bound * sharp(p)))
         e = jnp.exp(partition_affinity_bound * squash)
@@ -177,21 +179,21 @@
         squash_ref[:, cols] = squash
         weight[:, cols] = w
         weight_b[:, cols] = wb
-        mass[p : p + 1, :] = jnp.sum(w, axis=0, keepdims=True)
+        mass[i // 2, i % 2 : i % 2 + 1, :] = jnp.sum(w, axis=0, keepdims=True)
         tok = dot(wb, feature[:, cols], (0, 0))
         back = dot(wb, cot_ref[:, cols], (0, 0))
         both = jnp.where(half_mask, tok, swap(back))
-        part[p // 2, 2 * (p % 2) : 2 * (p % 2) + 2] = both.reshape(2, NZ, 8, LANES)
-
-    greeted()
-    copies = [
-        sends.start(part.at[other], rc, partner),
-        sends.start(mass, rcm, partner),
-    ]
+        part[core, 2 * (i % 2) : 2 * (i % 2) + 2] = both.reshape(2, NZ, 8, LANES)
+        if i == 1:
+            greeted()
+            copies = [
+                sends.start(part.at[other], rc, partner),
+                sends.start(mass.at[0], rcm, partner),
+            ]
     xt[...] = x_ref[...].T
     sends.recv(copies)
     s1[...] = part[at.c] + rc[...]
-    m1[...] = mass[...] + rcm[...]
+    m1[...] = mass[1] + rcm[...]
 
     copies = []
     for k, there, device in at.along("x"):
@@ -223,7 +225,7 @@
     sends.recv([sends.start(mine, mine, d) for _, _, d in at.along("z")])
 
     odd = lax.rem(at.x, 2)
-    pair = at.c * 2 + lax.div(at.x, 2)
+    pair = lax.div(at.x, 2)
     rows8 = lax.broadcasted_iota(jnp.int32, (8, LANES), 0)
     mass_row = jnp.sum(jnp.where(rows8 == pair, done[1], 0.0), axis=0, keepdims=True)
     r = lax.broadcasted_iota(jnp.int32, (WIDTH, LANES), 0)
@@ -457,7 +459,7 @@
             pltpu.VMEM((rows, width), F32),
             pltpu.VMEM((rows, width), BF16),
             f32(2, NX, NZ),
-            f32(),
+            f32(2),
             pltpu.VMEM((width, rows), BF16),
             f32(NZ, 2),
             pltpu.VMEM((NZ, rows, LANES), BF16),

time: 78.6 us -> 79.4 us (1.010)
  Pallas kernels: 77.8 us -> 78.6 us
    pallas_call x1, Pallas kernels: 75.9 us -> 76.8 us  [body(): pl.pallas_call(kernel, out_shape=(jax.ShapeDtypeStruct((rows, width), BF1...]
where the time goes in v5:
time: 79.4 us; the launch traced here: 79.3 us
  Pallas kernels  78.6 us (99%)
    pallas_call x1, Pallas kernels, body(): pl.pallas_call(kernel, out_shape=(jax.ShapeDtypeStruct((rows, width), BF1...  76.8 us
    pallas_call x1, Pallas kernels, body(): pl.pallas_call(store_kernel, out_shape=tuple((jax.ShapeDtypeStruct(r.shap...  1.82 us

profile of v5, /device:TPU:1, one launch (start us, length us, event | category | flops | bytes accessed | tf_op | source)
XLA Modules:
  0.0 79.3 jit_solution(95742783231428533)
XLA Ops:
  0.6 76.8 %layer.1 = (bf16[256,512]{1,0:T(8,128)(2,1)}, f32[16,1024]{1,0:T(8,128)}, f32[64,64]{1,0:T(8,128)}, f32[3,64,64]{2,1,0:T(8,128)}) custom-call(bf16[256,512]{1,0:T(8,128)(2,1)} %x_ref.1, bf16[512,512]{1,0:T(8,128)(2,1)} %we_ref.1, bf16[512,512]{1,0:T(8,128)(2,1)} %ws_ref.1, bf16[64,64]{1,0:T(8,128)(2,1)} %wa_ref.1, f32[8]{0:T(128)} %sharp_ref.1, ...), custom_call_target="tpu_custom_call" | custom-call | tf_op jit(solution)/shard_map/layer/pallas_call | solution.py:445
  77.4 1.8 %store.1 = (bf16[256,512]{1,0:T(8,128)(2,1)}, f32[16,1024]{1,0:T(8,128)}, f32[64,64]{1,0:T(8,128)}, f32[3,64,64]{2,1,0:T(8,128)}) custom-call(bf16[256,512]{1,0:T(8,128)(2,1)} %get-tuple-element.8.refs_0_, f32[16,1024]{1,0:T(8,128)} %get-tuple-element.9.refs_1_, f32[64,64]{1,0:T(8,128)} %get-tuple-element.10.refs_2_, f32[3,64,64]{2,1,0:T(8,128)} %get-tuple-element.11.refs_3_), custom_call_target="tpu_custom_call" | custom-call | tf_op jit(solution)/shard_map/store/pallas_call | solution.py:519
